TPU v7x, 256 devices: a whole 4x4x8 slice. The times are simulated.
256 devices in a mesh: dp: 8 (over z), expert: 32 (over y, x, core).
Axes of the slice: x: 4, y: 4, z: 8, core: 2. Of those that a mesh axis runs over, the one named last changes fastest.
Arguments:
- tokens: bfloat16 [32768, 2048], P(('dp', 'expert')), may hold values from -24 to 24
- expert_ids: int32 [32768, 2], P(('dp', 'expert')), may hold values from 0 to 31, as said below
- slot_index: int32 [32768, 2], P(('dp', 'expert')), may hold values from 0 to 15, as said below
- routing_gates: float32 [32768, 2], P(('dp', 'expert')), may hold values from 0.2 to 1
- grad_out: bfloat16 [32768, 2048], P(('dp', 'expert')), may hold values from -1.5 to 1.5
- w_gate: bfloat16 [32, 2048, 768], P('expert', 'dp'), may hold values from -0.125 to 0.125
- w_up: bfloat16 [32, 2048, 768], P('expert', 'dp'), may hold values from -0.125 to 0.125
- w_down: bfloat16 [32, 2048, 768], P('expert', 'dp'), may hold values from -0.21875 to 0.21875
Outputs:
- layer_out: bfloat16 [32768, 2048], P(('dp', 'expert'))
- grad_tokens: bfloat16 [32768, 2048], P(('dp', 'expert'))
- grad_gates: float32 [32768, 2], P(('dp', 'expert'))
- grad_w_gate: bfloat16 [32, 2048, 768], P('expert', 'dp')
- grad_w_up: bfloat16 [32, 2048, 768], P('expert', 'dp')
- grad_w_down: bfloat16 [32, 2048, 768], P('expert', 'dp')
Inputs may be any that keep to these rules, and one draw needn't show every extreme that they name: `expert_ids`: each row names 2 different experts. In each aligned block of 128 rows no expert is named more than 16 times; for each group of 32 blocks in a row, some expert is named exactly 16 times in every block of the group. `slot_index`: within one aligned block of 128 rows, the pairs that name one expert have distinct places, 0 up to their number minus one.
All inputs are finite; a program needn't handle non-finite values.
Results may differ from a plain program's by a relative error of at most 0.014.
Values may be sent and summed in bfloat16 or wider, within the bound.
A program may use at most 128 MiB of HBM per device.

v0:
```python
import jax
import jax.numpy as jnp
from jax import lax
from jax.sharding import PartitionSpec as P


def partial_term(left_rows, right_rows):
    return lax.dot_general(
        left_rows, right_rows, (((0,), (0,)), ((), ())), preferred_element_type=jnp.float32
    )


def on_device(tokens, expert_ids, slot_index, routing_gates, grad_out, w_gate, w_up, w_down):
    tok_dev, top_k = expert_ids.shape
    model_width = tokens.shape[1]
    experts = lax.axis_size("expert")
    capacity = 2 * tok_dev * top_k // experts
    target = (expert_ids * capacity + slot_index).reshape(-1)
    pair_index = jnp.arange(tok_dev * top_k, dtype=jnp.int32)
    source = jnp.full((experts * capacity,), -1, jnp.int32).at[target].set(pair_index)
    occupied = (source >= 0)[:, None]
    pair_safe = jnp.where(source >= 0, source, 0)
    token_safe = pair_safe // top_k
    zero_row = jnp.zeros((), jnp.bfloat16)
    outbound = jnp.where(occupied, tokens[token_safe], zero_row).reshape(
        experts, capacity, model_width
    )
    scaled = (routing_gates[:, :, None] * grad_out[:, None, :].astype(jnp.float32)).astype(
        jnp.bfloat16
    )
    scaled_rows = scaled.reshape(-1, model_width)
    grad_outbound = jnp.where(occupied, scaled_rows[pair_safe], zero_row).reshape(
        experts, capacity, model_width
    )
    gathered = (
        lax.all_gather(w_gate, "dp", axis=1, tiled=True),
        lax.all_gather(w_up, "dp", axis=1, tiled=True),
        lax.all_gather(w_down, "dp", axis=1, tiled=True),
    )
    full_gate = gathered[0][0]
    full_up = gathered[1][0]
    full_down = gathered[2][0]
    arrived = lax.all_to_all(outbound, "expert", split_axis=0, concat_axis=0, tiled=True)
    slot_count = arrived.shape[1]
    forward_flat_rows = arrived.reshape(-1, model_width)
    gate_pre = jnp.dot(forward_flat_rows, full_gate, preferred_element_type=jnp.float32)
    up_pre = jnp.dot(forward_flat_rows, full_up, preferred_element_type=jnp.float32)
    forward_hidden = (gate_pre * jax.nn.sigmoid(gate_pre) * up_pre).astype(jnp.bfloat16)
    produced = jnp.dot(forward_hidden, full_down.T, preferred_element_type=jnp.float32).astype(
        jnp.bfloat16
    )
    returned = lax.all_to_all(
        produced.reshape(experts, slot_count, model_width),
        "expert",
        split_axis=0,
        concat_axis=0,
        tiled=True,
    )
    returned, arrived, gate_stack, up_stack = (
        returned,
        arrived,
        gate_pre.reshape(experts, slot_count, -1),
        up_pre.reshape(experts, slot_count, -1),
    )
    grad_arrived = lax.all_to_all(grad_outbound, "expert", split_axis=0, concat_axis=0, tiled=True)
    by_pair = returned.reshape(-1, model_width)[target].reshape(tok_dev, top_k, model_width)
    layer_out = jnp.sum(by_pair.astype(jnp.float32) * routing_gates[:, :, None], axis=1).astype(
        jnp.bfloat16
    )
    grad_gates = jnp.einsum("tkd,td->tk", by_pair, grad_out, preferred_element_type=jnp.float32)
    flat_grad = grad_arrived.reshape(-1, model_width)
    flat_rows = arrived.reshape(-1, model_width)
    gate_flat = gate_stack.reshape(flat_grad.shape[0], -1)
    up_flat = up_stack.reshape(flat_grad.shape[0], -1)
    sigmoid_gate = jax.nn.sigmoid(gate_flat)
    active = gate_flat * sigmoid_gate
    hidden = (active * up_flat).astype(jnp.bfloat16)
    down_back = jnp.dot(flat_grad, full_down, preferred_element_type=jnp.float32)
    silu_slope = sigmoid_gate * (1.0 + gate_flat * (1.0 - sigmoid_gate))
    grad_gate_pre = (down_back * up_flat * silu_slope).astype(jnp.bfloat16)
    grad_up_pre = (down_back * active).astype(jnp.bfloat16)
    input_back = (
        jnp.dot(grad_gate_pre, full_gate.T, preferred_element_type=jnp.float32)
        + jnp.dot(grad_up_pre, full_up.T, preferred_element_type=jnp.float32)
    ).astype(jnp.bfloat16)
    input_return = lax.all_to_all(
        input_back.reshape(experts, capacity, model_width),
        "expert",
        split_axis=0,
        concat_axis=0,
        tiled=True,
    )
    back_pairs = input_return.reshape(-1, model_width)[target].reshape(tok_dev, top_k, model_width)
    grad_tokens = jnp.sum(back_pairs.astype(jnp.float32), axis=1).astype(jnp.bfloat16)
    grad_gate_w = lax.psum_scatter(
        partial_term(flat_rows, grad_gate_pre).astype(jnp.bfloat16),
        "dp",
        scatter_dimension=0,
        tiled=True,
    )
    grad_up_w = lax.psum_scatter(
        partial_term(flat_rows, grad_up_pre).astype(jnp.bfloat16),
        "dp",
        scatter_dimension=0,
        tiled=True,
    )
    grad_down_w = lax.psum_scatter(
        partial_term(flat_grad, hidden).astype(jnp.bfloat16), "dp", scatter_dimension=0, tiled=True
    )
    return (
        layer_out,
        grad_tokens,
        grad_gates,
        grad_gate_w[None],
        grad_up_w[None],
        grad_down_w[None],
    )


def solution(mesh):
    in_specs = (
        P(("dp", "expert"), None),
        P(("dp", "expert"), None),
        P(("dp", "expert"), None),
        P(("dp", "expert"), None),
        P(("dp", "expert"), None),
        P("expert", "dp", None),
        P("expert", "dp", None),
        P("expert", "dp", None),
    )
    out_specs = (
        P(("dp", "expert"), None),
        P(("dp", "expert"), None),
        P(("dp", "expert"), None),
        P("expert", "dp", None),
        P("expert", "dp", None),
        P("expert", "dp", None),
    )
    return jax.shard_map(
        on_device, mesh=mesh, in_specs=in_specs, out_specs=out_specs, check_vma=False
    )
```

profile of v0, /device:TPU:2, one launch (start us, length us, event | category | flops | bytes accessed | tf_op | source)
XLA Modules:
  0.0 312.3 jit_solution(7386118729877439063)
XLA Ops:
  7.2 0.7 all-gather.8.cloned.1.call-update
  7.9 0.0 all-gather.6.cloned.1.call-start
  8.0 0.7 all-gather.6.cloned.1.call-update
  8.7 0.0 all-gather.4.cloned.1.call-start
  8.7 0.7 all-gather.4.cloned.1.call-update
  9.4 2.1 mul.63
  11.5 2.5 mul.64
  14.0 0.1 copy.16
  14.1 0.1 mul.61
  14.3 0.1 copy.15
  14.4 0.1 reshape.88
  14.5 1.4 scatter_custom_fusion
  16.0 0.1 broadcast_in_dim.46
  16.0 1.8 multiply_convert_fusion
  17.9 3.3 %gather_fusion.2 = bf16[512,2048]{1,0:T(8,128)(2,1)} fusion(bf16[256,2048]{1,0:T(8,128)(2,1)S(1)} %multiply_convert_fusion, s32[1024]{0:T(1024)S(1)} %get-tuple-element.13), kind=kCustom, calls=%fused_computation.2 | custom fusion | bytes 4196352 | tf_op jit(solution)/shard_map/gather | solution.py:32
  21.2 3.3 %gather_fusion = bf16[512,2048]{1,0:T(8,128)(2,1)} fusion(bf16[128,2048]{1,0:T(8,128)(2,1)S(1)} %copy-done, s32[1024]{0:T(1024)S(1)} %get-tuple-element.14), kind=kCustom, calls=%fused_computation | custom fusion | bytes 4196352 | tf_op jit(solution)/shard_map/gather | solution.py:25
  24.5 3.2 %broadcast_select_fusion = (bf16[32,16,2048]{2,1,0:T(8,128)(2,1)S(1)}, bf16[32,16,2048]{2,1,0:T(8,128)(2,1)}) fusion(bf16[32,16,2048]{2,1,0:T(8,128)(2,1)S(1)} %bitcast.49, pred[32,16]{1,0:T(8,128)(4,1)S(1)} %broadcast_in_dim.46, bf16[32,16,2048]{2,1,0:T(8,128)(2,1)} %bitcast.50), kind=kLoop, calls=%fused_computation.24 | loop fusion | flops 2097152 | bytes 8389120 | tf_op jit(solution)/shard_map/jit(_where)/select_n | solution.py:32
  27.7 34.6 %all_to_all.20 = bf16[32,16,2048]{2,1,0:T(8,128)(2,1)S(1)} all-to-all(bf16[32,16,2048]{2,1,0:T(8,128)(2,1)S(1)} %get-tuple-element.9), channel_id=1, replica_groups=mesh['dp'=8,'expert'=32] {'expert'}, dimensions={0} | all-to-all | bytes 4194304 | tf_op jit(solution)/shard_map/all_to_all | solution.py:65
  62.4 5.8 %all-to-all-start = ((bf16[32,16,2048]{2,1,0:T(8,128)(2,1)}), bf16[32,16,2048]{2,1,0:T(8,128)(2,1)}, u32[]{:S(2)}, u32[]{:S(2)}) async-start(bf16[32,16,2048]{2,1,0:T(8,128)(2,1)} %get-tuple-element.10), calls=%async_computation | async-start | bytes 4194304 | tf_op jit(solution)/shard_map/all_to_all | solution.py:43
  68.2 0.2 reduce-scatter.4.cloned.1.call-start
  68.4 5.1 %fusion = f32[512,768]{1,0:T(8,128)} fusion(bf16[512,2048]{1,0:T(8,128)(2,1)S(1)} %bitcast.51, bf16[1,2048,768]{2,1,0:T(8,128)(2,1)} %all-gather.8.cloned.1.call-done), kind=kOutput, calls=%fused_computation.9 | convolution fusion | flops 1610612736 | bytes 6815744 | tf_op jit(solution)/shard_map/dot_general | solution.py:78
  73.5 22.8 %all-to-all-done = bf16[32,16,2048]{2,1,0:T(8,128)(2,1)} async-done(((bf16[32,16,2048]{2,1,0:T(8,128)(2,1)}), bf16[32,16,2048]{2,1,0:T(8,128)(2,1)}, u32[]{:S(2)}, u32[]{:S(2)}) %all-to-all-start) | async-done | bytes 2097184 | tf_op jit(solution)/shard_map/all_to_all | solution.py:43
  96.3 6.9 %all-gather.6.cloned.1.call-done = bf16[1,2048,768]{2,1,0:T(8,128)(2,1)} async-done(((bf16[1,256,768]{2,1,0:T(8,128)(2,1)}), bf16[1,2048,768]{2,1,0:T(8,128)(2,1)}) %all-gather.6.cloned.1.call-update) | async-done | bytes 3145744 | tf_op jit(solution)/shard_map/all_gather | solution.py:37
  103.2 5.4 %fusion.6 = f32[512,768]{1,0:T(8,128)} fusion(bf16[512,2048]{1,0:T(8,128)(2,1)} %bitcast.2, bf16[1,2048,768]{2,1,0:T(8,128)(2,1)} %all-gather.6.cloned.1.call-done), kind=kOutput, calls=%fused_computation.15 | convolution fusion | flops 1610612736 | bytes 6815744 | tf_op jit(solution)/shard_map/dot_general | solution.py:47
  108.6 40.0 %all-gather.4.cloned.1.call-done = bf16[1,2048,768]{2,1,0:T(8,128)(2,1)} async-done(((bf16[1,256,768]{2,1,0:T(8,128)(2,1)}), bf16[1,2048,768]{2,1,0:T(8,128)(2,1)}) %all-gather.4.cloned.1.call-update) | async-done | bytes 3145744 | tf_op jit(solution)/shard_map/all_gather | solution.py:36
  148.6 6.9 %multiply_convert_fusion.2 = (bf16[512,768]{1,0:T(8,128)(2,1)S(1)}, bf16[512,768]{1,0:T(8,128)(2,1)}, bf16[512,768]{1,0:T(8,128)(2,1)}) fusion(f32[512,768]{1,0:T(8,128)} %fusion, f32[512,768]{1,0:T(8,128)} %fusion.6, bf16[512,2048]{1,0:T(8,128)(2,1)} %bitcast.2, bf16[1,2048,768]{2,1,0:T(8,128)(2,1)} %all-gather.4.cloned.1.call-done), kind=kOutput, calls=%fused_computation.27 | convolution fusion | flops 1616510976 | bytes 10747904 | tf_op jit(solution)/shard_map/dot_general | solution.py:46
  155.5 5.1 %convolution_convert_fusion.2 = bf16[2048,768]{1,0:T(8,128)(2,1)} fusion(bf16[512,2048]{1,0:T(8,128)(2,1)} %bitcast.2, bf16[512,768]{1,0:T(8,128)(2,1)S(1)} %get-tuple-element.6), kind=kOutput, calls=%fused_computation.8 | convolution fusion | flops 1612185600 | bytes 6029312 | tf_op jit(solution)/shard_map/dot_general | solution.py:8
  160.7 0.0 reduce-scatter.6.cloned.1.call-start
  160.7 5.2 %convolution_convert_fusion.1 = bf16[2048,768]{1,0:T(8,128)(2,1)} fusion(bf16[512,2048]{1,0:T(8,128)(2,1)} %bitcast.2, bf16[512,768]{1,0:T(8,128)(2,1)} %get-tuple-element.7), kind=kOutput, calls=%fused_computation.7 | convolution fusion | flops 1612185600 | bytes 6029312 | tf_op jit(solution)/shard_map/dot_general | solution.py:8
  166.0 0.0 reduce-scatter.8.cloned.1.call-start
  166.0 4.6 %convolution_convert_fusion = bf16[2048,768]{1,0:T(8,128)(2,1)} fusion(bf16[512,2048]{1,0:T(8,128)(2,1)S(1)} %bitcast.52, bf16[512,768]{1,0:T(8,128)(2,1)} %get-tuple-element.8), kind=kOutput, calls=%fused_computation.6 | convolution fusion | flops 1612185600 | bytes 6029312 | tf_op jit(solution)/shard_map/dot_general | solution.py:8
  170.7 1.1 copy-done.8
  171.8 5.0 %fusion.12 = bf16[512,2048]{1,0:T(8,128)(2,1)} fusion(bf16[512,768]{1,0:T(8,128)(2,1)S(1)} %copy-done.8, bf16[1,2048,768]{2,1,0:T(8,128)(2,1)} %all-gather.8.cloned.1.call-done), kind=kOutput, calls=%fused_computation.21 | convolution fusion | flops 1611661312 | bytes 6029312 | tf_op jit(solution)/shard_map/dot_general | solution.py:49
  176.8 7.4 %all-to-all-start.1 = ((bf16[32,16,2048]{2,1,0:T(8,128)(2,1)}), bf16[32,16,2048]{2,1,0:T(8,128)(2,1)S(1)}, u32[]{:S(2)}, u32[]{:S(2)}) async-start(bf16[32,16,2048]{2,1,0:T(8,128)(2,1)} %bitcast.54), calls=%async_computation.1 | async-start | bytes 4194304 | tf_op jit(solution)/shard_map/all_to_all | solution.py:52
  184.3 4.1 %fusion.4 = f32[512,2048]{1,0:T(8,128)S(1)} fusion(bf16[512,768]{1,0:T(8,128)(2,1)} %get-tuple-element.7, bf16[1,2048,768]{2,1,0:T(8,128)(2,1)} %all-gather.6.cloned.1.call-done), kind=kOutput, calls=%fused_computation.13 | convolution fusion | flops 1610612736 | bytes 8126464 | tf_op jit(solution)/shard_map/dot_general | solution.py:84
  188.4 3.2 %add_convert_fusion = bf16[512,2048]{1,0:T(8,128)(2,1)} fusion(f32[512,2048]{1,0:T(8,128)S(1)} %fusion.4, bf16[512,768]{1,0:T(8,128)(2,1)S(1)} %get-tuple-element.6, bf16[1,2048,768]{2,1,0:T(8,128)(2,1)S(1)} %copy-done.7), kind=kOutput, calls=%fused_computation.5 | convolution fusion | flops 1612709888 | bytes 10223616 | tf_op jit(solution)/shard_map/dot_general | solution.py:83
  191.6 20.6 %all-to-all-done.1 = bf16[32,16,2048]{2,1,0:T(8,128)(2,1)S(1)} async-done(((bf16[32,16,2048]{2,1,0:T(8,128)(2,1)}), bf16[32,16,2048]{2,1,0:T(8,128)(2,1)S(1)}, u32[]{:S(2)}, u32[]{:S(2)}) %all-to-all-start.1) | async-done | bytes 2097184 | tf_op jit(solution)/shard_map/all_to_all | solution.py:52
  212.2 6.7 %all-to-all-start.3 = ((bf16[32,16,2048]{2,1,0:T(8,128)(2,1)}), bf16[32,16,2048]{2,1,0:T(8,128)(2,1)}, u32[]{:S(2)}, u32[]{:S(2)}) async-start(bf16[32,16,2048]{2,1,0:T(8,128)(2,1)} %bitcast.53), calls=%async_computation.3 | async-start | bytes 4194304 | tf_op jit(solution)/shard_map/all_to_all | solution.py:86
  219.0 2.3 gather_fusion.1
  221.3 1.7 reshape.92
  223.0 24.0 %all-to-all-done.3 = bf16[32,16,2048]{2,1,0:T(8,128)(2,1)} async-done(((bf16[32,16,2048]{2,1,0:T(8,128)(2,1)}), bf16[32,16,2048]{2,1,0:T(8,128)(2,1)}, u32[]{:S(2)}, u32[]{:S(2)}) %all-to-all-start.3) | async-done | bytes 2097184 | tf_op jit(solution)/shard_map/all_to_all | solution.py:86
  247.0 4.2 %gather_fusion.3 = bf16[256,2048]{1,0:T(8,128)(2,1)S(1)} fusion(bf16[512,2048]{1,0:T(8,128)(2,1)} %bitcast.11, s32[1024]{0:T(1024)S(1)} %pad_clamp_fusion.1), kind=kCustom, calls=%fused_computation.3 | custom fusion | bytes 2098176 | tf_op jit(solution)/shard_map/gather | solution.py:93
  251.3 1.5 reshape.96
  252.8 2.3 fusion.18
  255.1 0.7 copy.19
  255.8 3.6 %reduce_sum.22 = bf16[128,2048]{1,0:T(8,128)(2,1)} reduce(bf16[128,2,2048]{2,1,0:T(2,128)(2,1)S(1)} %copy-done.2, bf16[]{:T(256)} %constant.29.clone.1), dimensions={1}, to_apply=%region_2.3 | reduce | flops 262144 | bytes 1572866 | tf_op jit(solution)/shard_map/reduce_sum | solution.py:94
  259.4 3.9 %multiply_reduce_fusion = bf16[128,2048]{1,0:T(8,128)(2,1)} fusion(bf16[128,2,2048]{2,1,0:T(2,128)(2,1)S(1)} %reshape.92, f32[128,2]{1,0:T(8,128)S(1)} %copy.16), kind=kLoop, calls=%fused_computation.23 | loop fusion | flops 1310720 | bytes 1573888 | tf_op jit(solution)/shard_map/reduce_sum | solution.py:67
  263.3 42.2 %reduce-scatter.8.cloned.1.call-done = bf16[256,768]{1,0:T(8,128)(2,1)} async-done(((bf16[2048,768]{1,0:T(8,128)(2,1)}), bf16[256,768]{1,0:T(8,128)(2,1)}) %reduce-scatter.8.cloned.1.call-update) | async-done | bytes 393232 | tf_op jit(solution)/shard_map/reduce_scatter | solution.py:107
  (31 shorter events, 0.2 us)
Async XLA Ops:
  7.2 14.0 %copy-start = (bf16[128,2048]{1,0:T(8,128)(2,1)S(1)}, bf16[128,2048]{1,0:T(8,128)(2,1)}, u32[]{:S(2)}) copy-start(bf16[128,2048]{1,0:T(8,128)(2,1)} %param.8) | copy-start | bytes 1572868
  7.2 61.3 %all-gather.8.cloned.1.call-start = ((), (), s32[]{:S(2)}) async-start(), calls=%async_computation.9 | async-start | bytes 3538944 | tf_op jit(solution)/shard_map/all_gather | solution.py:38
  7.9 95.3 %all-gather.6.cloned.1.call-start = ((), (), s32[]{:S(2)}) async-start(), calls=%async_computation.8 | async-start | bytes 3538944 | tf_op jit(solution)/shard_map/all_gather | solution.py:37
  8.7 140.0 %all-gather.4.cloned.1.call-start = ((), (), s32[]{:S(2)}) async-start(), calls=%async_computation.7 | async-start | bytes 3538944 | tf_op jit(solution)/shard_map/all_gather | solution.py:36
  11.5 2.5 copy-start.4
  11.5 2.7 copy-start.5
  11.5 2.7 copy-start.6
  21.2 3.3 %copy-start.1 = (bf16[512,2048]{1,0:T(8,128)(2,1)S(1)}, bf16[512,2048]{1,0:T(8,128)(2,1)}, u32[]{:S(2)}) copy-start(bf16[512,2048]{1,0:T(8,128)(2,1)} %gather_fusion.2) | copy-start | bytes 6291460
  62.4 33.9 %all-to-all-start = ((bf16[32,16,2048]{2,1,0:T(8,128)(2,1)}), bf16[32,16,2048]{2,1,0:T(8,128)(2,1)}, u32[]{:S(2)}, u32[]{:S(2)}) async-start(bf16[32,16,2048]{2,1,0:T(8,128)(2,1)} %get-tuple-element.10), calls=%async_computation | async-start | bytes 4194304 | tf_op jit(solution)/shard_map/all_to_all | solution.py:43
  68.2 195.1 %reduce-scatter.4.cloned.1.call-start = ((), (), s32[]{:S(2)}) async-start(), calls=%async_computation.10 | async-start | bytes 3538944 | tf_op jit(solution)/shard_map/reduce_scatter | solution.py:95
  160.7 102.6 %reduce-scatter.6.cloned.1.call-start = ((), (), s32[]{:S(2)}) async-start(), calls=%async_computation.11 | async-start | bytes 3538944 | tf_op jit(solution)/shard_map/reduce_scatter | solution.py:101
  166.0 139.5 %reduce-scatter.8.cloned.1.call-start = ((), (), s32[]{:S(2)}) async-start(), calls=%async_computation.12 | async-start | bytes 3538944 | tf_op jit(solution)/shard_map/reduce_scatter | solution.py:107
  170.7 1.2 copy-start.8
  176.8 35.3 %all-to-all-start.1 = ((bf16[32,16,2048]{2,1,0:T(8,128)(2,1)}), bf16[32,16,2048]{2,1,0:T(8,128)(2,1)S(1)}, u32[]{:S(2)}, u32[]{:S(2)}) async-start(bf16[32,16,2048]{2,1,0:T(8,128)(2,1)} %bitcast.54), calls=%async_computation.1 | async-start | bytes 4194304 | tf_op jit(solution)/shard_map/all_to_all | solution.py:52
  184.3 4.1 %copy-start.7 = (bf16[1,2048,768]{2,1,0:T(8,128)(2,1)S(1)}, bf16[1,2048,768]{2,1,0:T(8,128)(2,1)}, u32[]{:S(2)}) copy-start(bf16[1,2048,768]{2,1,0:T(8,128)(2,1)} %all-gather.4.cloned.1.call-done) | copy-start | bytes 9437188
  212.2 34.8 %all-to-all-start.3 = ((bf16[32,16,2048]{2,1,0:T(8,128)(2,1)}), bf16[32,16,2048]{2,1,0:T(8,128)(2,1)}, u32[]{:S(2)}, u32[]{:S(2)}) async-start(bf16[32,16,2048]{2,1,0:T(8,128)(2,1)} %bitcast.53), calls=%async_computation.3 | async-start | bytes 4194304 | tf_op jit(solution)/shard_map/all_to_all | solution.py:86
  251.3 1.5 copy-start.3
  252.8 3.0 copy-start.2
Sparse Core Ops, SparseCore 0:
  9.8 47.9 all-gather.7
  59.5 43.6 all-gather.5
  105.0 43.5 all-gather.3
  160.8 45.7 reduce-scatter.3
  209.5 46.2 reduce-scatter.5
  258.8 46.5 reduce-scatter.7
where the time goes:
time: 313 us; the launch traced here: 312 us
  waiting for transfers between devices  159 us (51%)
  matrix products  47 us (15%)
  blocking collectives  34.6 us (11%)
  local copies, waits for them, and re-layouts  24.8 us (8%)
  starting transfers between devices  20.4 us (7%)
  between operations  14.3 us (5%)
  other arithmetic  12.5 us (4%)
    reduce_scatter x1, waiting for transfers between devices, on_device(): lax.psum_scatter(partial_term(flat_grad, hidden).astype(jnp.bfloat16), 'd...  42.2 us
    all_gather x1, waiting for transfers between devices, on_device(): lax.all_gather(w_gate, 'dp', axis=1, tiled=True)  40 us
    all_to_all x1, blocking collectives, on_device(): lax.all_to_all(grad_outbound, 'expert', split_axis=0, concat_axis=0, tile...  34.6 us
    all_to_all x1, waiting for transfers between devices, on_device(): lax.all_to_all(input_back.reshape(experts, capacity, model_width), 'exper...  24 us
    all_to_all x1, waiting for transfers between devices, on_device(): lax.all_to_all(outbound, 'expert', split_axis=0, concat_axis=0, tiled=True)  22.8 us
    all_to_all x1, waiting for transfers between devices, on_device(): lax.all_to_all(produced.reshape(experts, slot_count, model_width), 'exper...  20.6 us
    dot_general x3, matrix products, partial_term(): lax.dot_general(left_rows, right_rows, (((0,), (0,)), ((), ())), preferre...  15 us
    all_to_all x1, starting transfers between devices, on_device(): lax.all_to_all(produced.reshape(experts, slot_count, model_width), 'exper...  7.43 us
  transfers between devices with their start and end apart: 9, of which 6 were waited for; matrix products, arithmetic and copies ran while one was open for 23% of the time, Pallas kernels for 0%

commit v1 on v0

--- a/solution.py
+++ b/solution.py
@@ -33,7 +33,7 @@
         experts, capacity, model_width
     )
     gathered = (
-        lax.all_gather(w_gate, "dp", axis=1, tiled=True),
+        jnp.concatenate(lax.all_gather(w_gate, "dp"), axis=1),
         lax.all_gather(w_up, "dp", axis=1, tiled=True),
         lax.all_gather(w_down, "dp", axis=1, tiled=True),
     )

time: 313 us -> 313 us (level)
  no operation moved by 1% of the time
where the time goes in v1:
time: 313 us; the launch traced here: 312 us
  waiting for transfers between devices  159 us (51%)
  matrix products  47 us (15%)
  blocking collectives  34.6 us (11%)
  local copies, waits for them, and re-layouts  24.8 us (8%)
  starting transfers between devices  20.4 us (7%)
  between operations  14.3 us (5%)
  other arithmetic  12.5 us (4%)
    reduce_scatter x1, waiting for transfers between devices, on_device(): lax.psum_scatter(partial_term(flat_grad, hidden).astype(jnp.bfloat16), 'd...  42.2 us
    all_gather x1, waiting for transfers between devices, on_device(): lax.all_gather(w_gate, 'dp')  40 us
    all_to_all x1, blocking collectives, on_device(): lax.all_to_all(grad_outbound, 'expert', split_axis=0, concat_axis=0, tile...  34.6 us
    all_to_all x1, waiting for transfers between devices, on_device(): lax.all_to_all(input_back.reshape(experts, capacity, model_width), 'exper...  24 us
    all_to_all x1, waiting for transfers between devices, on_device(): lax.all_to_all(outbound, 'expert', split_axis=0, concat_axis=0, tiled=True)  22.8 us
    all_to_all x1, waiting for transfers between devices, on_device(): lax.all_to_all(produced.reshape(experts, slot_count, model_width), 'exper...  20.6 us
    dot_general x3, matrix products, partial_term(): lax.dot_general(left_rows, right_rows, (((0,), (0,)), ((), ())), preferre...  15 us
    all_to_all x1, starting transfers between devices, on_device(): lax.all_to_all(produced.reshape(experts, slot_count, model_width), 'exper...  7.43 us
  transfers between devices with their start and end apart: 9, of which 6 were waited for; matrix products, arithmetic and copies ran while one was open for 23% of the time, Pallas kernels for 0%

profile of v1, /device:TPU:2, one launch (start us, length us, event | category | flops | bytes accessed | tf_op | source)
XLA Modules:
  0.0 312.3 jit_solution(8542649261559341164)
XLA Ops:
  7.2 0.7 all-gather.7.cloned.1.call-update
  7.9 0.0 all-gather.5.cloned.1.call-start
  8.0 0.7 all-gather.5.cloned.1.call-update
  8.7 0.0 all-gather.9.cloned.1.call-start
  8.7 0.7 all-gather.9.cloned.1.call-update
  9.4 2.1 mul.63
  11.5 2.5 mul.64
  14.0 0.1 copy.19
  14.1 0.1 mul.61
  14.3 0.1 copy.18
  14.4 0.1 reshape.88
  14.5 1.4 scatter_custom_fusion
  16.0 0.1 broadcast_in_dim.46
  16.0 1.8 multiply_convert_fusion
  17.9 3.3 %gather_fusion.2 = bf16[512,2048]{1,0:T(8,128)(2,1)} fusion(bf16[256,2048]{1,0:T(8,128)(2,1)S(1)} %multiply_convert_fusion, s32[1024]{0:T(1024)S(1)} %get-tuple-element.13), kind=kCustom, calls=%fused_computation.2 | custom fusion | bytes 4196352 | tf_op jit(solution)/shard_map/gather | solution.py:32
  21.2 3.3 %gather_fusion = bf16[512,2048]{1,0:T(8,128)(2,1)} fusion(bf16[128,2048]{1,0:T(8,128)(2,1)S(1)} %copy-done, s32[1024]{0:T(1024)S(1)} %get-tuple-element.14), kind=kCustom, calls=%fused_computation | custom fusion | bytes 4196352 | tf_op jit(solution)/shard_map/gather | solution.py:25
  24.5 3.2 %broadcast_select_fusion = (bf16[32,16,2048]{2,1,0:T(8,128)(2,1)S(1)}, bf16[32,16,2048]{2,1,0:T(8,128)(2,1)}) fusion(bf16[32,16,2048]{2,1,0:T(8,128)(2,1)S(1)} %bitcast.43, pred[32,16]{1,0:T(8,128)(4,1)S(1)} %broadcast_in_dim.46, bf16[32,16,2048]{2,1,0:T(8,128)(2,1)} %bitcast.44), kind=kLoop, calls=%fused_computation.20 | loop fusion | flops 2097152 | bytes 8389120 | tf_op jit(solution)/shard_map/jit(_where)/select_n | solution.py:32
  27.7 34.6 %all_to_all.20 = bf16[32,16,2048]{2,1,0:T(8,128)(2,1)S(1)} all-to-all(bf16[32,16,2048]{2,1,0:T(8,128)(2,1)S(1)} %get-tuple-element.9), channel_id=1, replica_groups=mesh['dp'=8,'expert'=32] {'expert'}, dimensions={0} | all-to-all | bytes 4194304 | tf_op jit(solution)/shard_map/all_to_all | solution.py:65
  62.4 5.8 %all-to-all-start = ((bf16[32,16,2048]{2,1,0:T(8,128)(2,1)}), bf16[32,16,2048]{2,1,0:T(8,128)(2,1)}, u32[]{:S(2)}, u32[]{:S(2)}) async-start(bf16[32,16,2048]{2,1,0:T(8,128)(2,1)} %get-tuple-element.10), calls=%async_computation | async-start | bytes 4194304 | tf_op jit(solution)/shard_map/all_to_all | solution.py:43
  68.2 0.2 reduce-scatter.4.cloned.1.call-start
  68.4 5.1 %fusion = f32[512,768]{1,0:T(8,128)} fusion(bf16[512,2048]{1,0:T(8,128)(2,1)S(1)} %bitcast.45, bf16[1,2048,768]{2,1,0:T(8,128)(2,1)} %all-gather.7.cloned.1.call-done), kind=kOutput, calls=%fused_computation.9 | convolution fusion | flops 1610612736 | bytes 6815744 | tf_op jit(solution)/shard_map/dot_general | solution.py:78
  73.5 22.8 %all-to-all-done = bf16[32,16,2048]{2,1,0:T(8,128)(2,1)} async-done(((bf16[32,16,2048]{2,1,0:T(8,128)(2,1)}), bf16[32,16,2048]{2,1,0:T(8,128)(2,1)}, u32[]{:S(2)}, u32[]{:S(2)}) %all-to-all-start) | async-done | bytes 2097184 | tf_op jit(solution)/shard_map/all_to_all | solution.py:43
  96.3 6.9 %all-gather.5.cloned.1.call-done = bf16[1,2048,768]{2,1,0:T(8,128)(2,1)} async-done(((bf16[1,256,768]{2,1,0:T(8,128)(2,1)}), bf16[1,2048,768]{2,1,0:T(8,128)(2,1)}) %all-gather.5.cloned.1.call-update) | async-done | bytes 3145744 | tf_op jit(solution)/shard_map/all_gather | solution.py:37
  103.2 5.4 %fusion.6 = f32[512,768]{1,0:T(8,128)} fusion(bf16[512,2048]{1,0:T(8,128)(2,1)} %bitcast.2, bf16[1,2048,768]{2,1,0:T(8,128)(2,1)} %all-gather.5.cloned.1.call-done), kind=kOutput, calls=%fused_computation.15 | convolution fusion | flops 1610612736 | bytes 6815744 | tf_op jit(solution)/shard_map/dot_general | solution.py:47
  108.6 40.0 %all-gather.9.cloned.1.call-done = bf16[8,256,768]{2,1,0:T(8,128)(2,1)} async-done(((bf16[1,256,768]{2,1,0:T(8,128)(2,1)}), bf16[8,256,768]{2,1,0:T(8,128)(2,1)}) %all-gather.9.cloned.1.call-update) | async-done | bytes 3145744 | tf_op jit(solution)/shard_map/all_gather | solution.py:36
  148.6 6.9 %multiply_convert_fusion.2 = (bf16[512,768]{1,0:T(8,128)(2,1)S(1)}, bf16[512,768]{1,0:T(8,128)(2,1)}, bf16[512,768]{1,0:T(8,128)(2,1)}) fusion(f32[512,768]{1,0:T(8,128)} %fusion, f32[512,768]{1,0:T(8,128)} %fusion.6, bf16[512,2048]{1,0:T(8,128)(2,1)} %bitcast.2, bf16[2048,768]{1,0:T(8,128)(2,1)} %bitcast.53), kind=kOutput, calls=%fused_computation.23 | convolution fusion | flops 1616510976 | bytes 10747904 | tf_op jit(solution)/shard_map/dot_general | solution.py:46
  155.5 5.1 %convolution_convert_fusion.2 = bf16[2048,768]{1,0:T(8,128)(2,1)} fusion(bf16[512,2048]{1,0:T(8,128)(2,1)} %bitcast.2, bf16[512,768]{1,0:T(8,128)(2,1)S(1)} %get-tuple-element.6), kind=kOutput, calls=%fused_computation.8 | convolution fusion | flops 1612185600 | bytes 6029312 | tf_op jit(solution)/shard_map/dot_general | solution.py:8
  160.7 0.0 reduce-scatter.6.cloned.1.call-start
  160.7 5.2 %convolution_convert_fusion.1 = bf16[2048,768]{1,0:T(8,128)(2,1)} fusion(bf16[512,2048]{1,0:T(8,128)(2,1)} %bitcast.2, bf16[512,768]{1,0:T(8,128)(2,1)} %get-tuple-element.7), kind=kOutput, calls=%fused_computation.7 | convolution fusion | flops 1612185600 | bytes 6029312 | tf_op jit(solution)/shard_map/dot_general | solution.py:8
  166.0 0.0 reduce-scatter.8.cloned.1.call-start
  166.0 4.6 %convolution_convert_fusion = bf16[2048,768]{1,0:T(8,128)(2,1)} fusion(bf16[512,2048]{1,0:T(8,128)(2,1)S(1)} %bitcast.46, bf16[512,768]{1,0:T(8,128)(2,1)} %get-tuple-element.8), kind=kOutput, calls=%fused_computation.6 | convolution fusion | flops 1612185600 | bytes 6029312 | tf_op jit(solution)/shard_map/dot_general | solution.py:8
  170.7 1.1 copy-done.8
  171.8 5.0 %fusion.8 = bf16[512,2048]{1,0:T(8,128)(2,1)} fusion(bf16[512,768]{1,0:T(8,128)(2,1)S(1)} %copy-done.8, bf16[1,2048,768]{2,1,0:T(8,128)(2,1)} %all-gather.7.cloned.1.call-done), kind=kOutput, calls=%fused_computation.17 | convolution fusion | flops 1611661312 | bytes 6029312 | tf_op jit(solution)/shard_map/dot_general | solution.py:49
  176.8 7.4 %all-to-all-start.1 = ((bf16[32,16,2048]{2,1,0:T(8,128)(2,1)}), bf16[32,16,2048]{2,1,0:T(8,128)(2,1)S(1)}, u32[]{:S(2)}, u32[]{:S(2)}) async-start(bf16[32,16,2048]{2,1,0:T(8,128)(2,1)} %bitcast.48), calls=%async_computation.1 | async-start | bytes 4194304 | tf_op jit(solution)/shard_map/all_to_all | solution.py:52
  184.3 4.1 %fusion.4 = f32[512,2048]{1,0:T(8,128)S(1)} fusion(bf16[512,768]{1,0:T(8,128)(2,1)} %get-tuple-element.7, bf16[1,2048,768]{2,1,0:T(8,128)(2,1)} %all-gather.5.cloned.1.call-done), kind=kOutput, calls=%fused_computation.13 | convolution fusion | flops 1610612736 | bytes 8126464 | tf_op jit(solution)/shard_map/dot_general | solution.py:84
  188.4 3.2 %add_convert_fusion = bf16[512,2048]{1,0:T(8,128)(2,1)} fusion(f32[512,2048]{1,0:T(8,128)S(1)} %fusion.4, bf16[512,768]{1,0:T(8,128)(2,1)S(1)} %get-tuple-element.6, bf16[2048,768]{1,0:T(8,128)(2,1)S(1)} %bitcast.54), kind=kOutput, calls=%fused_computation.5 | convolution fusion | flops 1612709888 | bytes 10223616 | tf_op jit(solution)/shard_map/dot_general | solution.py:83
  191.6 20.6 %all-to-all-done.1 = bf16[32,16,2048]{2,1,0:T(8,128)(2,1)S(1)} async-done(((bf16[32,16,2048]{2,1,0:T(8,128)(2,1)}), bf16[32,16,2048]{2,1,0:T(8,128)(2,1)S(1)}, u32[]{:S(2)}, u32[]{:S(2)}) %all-to-all-start.1) | async-done | bytes 2097184 | tf_op jit(solution)/shard_map/all_to_all | solution.py:52
  212.2 6.7 %all-to-all-start.3 = ((bf16[32,16,2048]{2,1,0:T(8,128)(2,1)}), bf16[32,16,2048]{2,1,0:T(8,128)(2,1)}, u32[]{:S(2)}, u32[]{:S(2)}) async-start(bf16[32,16,2048]{2,1,0:T(8,128)(2,1)} %bitcast.47), calls=%async_computation.3 | async-start | bytes 4194304 | tf_op jit(solution)/shard_map/all_to_all | solution.py:86
  218.9 2.3 gather_fusion.1
  221.3 1.7 reshape.92
  223.0 24.0 %all-to-all-done.3 = bf16[32,16,2048]{2,1,0:T(8,128)(2,1)} async-done(((bf16[32,16,2048]{2,1,0:T(8,128)(2,1)}), bf16[32,16,2048]{2,1,0:T(8,128)(2,1)}, u32[]{:S(2)}, u32[]{:S(2)}) %all-to-all-start.3) | async-done | bytes 2097184 | tf_op jit(solution)/shard_map/all_to_all | solution.py:86
  247.0 4.3 %gather_fusion.3 = bf16[256,2048]{1,0:T(8,128)(2,1)S(1)} fusion(bf16[512,2048]{1,0:T(8,128)(2,1)} %bitcast.11, s32[1024]{0:T(1024)S(1)} %pad_clamp_fusion.1), kind=kCustom, calls=%fused_computation.3 | custom fusion | bytes 2098176 | tf_op jit(solution)/shard_map/gather | solution.py:93
  251.3 1.5 reshape.96
  252.8 2.3 fusion.12
  255.1 0.7 copy.22
  255.8 3.6 %reduce_sum.22 = bf16[128,2048]{1,0:T(8,128)(2,1)} reduce(bf16[128,2,2048]{2,1,0:T(2,128)(2,1)S(1)} %copy-done.2, bf16[]{:T(256)} %constant.29.clone.1), dimensions={1}, to_apply=%region_2.3 | reduce | flops 262144 | bytes 1572866 | tf_op jit(solution)/shard_map/reduce_sum | solution.py:94
  259.4 3.9 %multiply_reduce_fusion = bf16[128,2048]{1,0:T(8,128)(2,1)} fusion(bf16[128,2,2048]{2,1,0:T(2,128)(2,1)S(1)} %reshape.92, f32[128,2]{1,0:T(8,128)S(1)} %copy.19), kind=kLoop, calls=%fused_computation.19 | loop fusion | flops 1310720 | bytes 1573888 | tf_op jit(solution)/shard_map/reduce_sum | solution.py:67
  263.3 42.2 %reduce-scatter.8.cloned.1.call-done = bf16[256,768]{1,0:T(8,128)(2,1)} async-done(((bf16[2048,768]{1,0:T(8,128)(2,1)}), bf16[256,768]{1,0:T(8,128)(2,1)}) %reduce-scatter.8.cloned.1.call-update) | async-done | bytes 393232 | tf_op jit(solution)/shard_map/reduce_scatter | solution.py:107
  (31 shorter events, 0.2 us)
Async XLA Ops:
  7.2 14.0 %copy-start = (bf16[128,2048]{1,0:T(8,128)(2,1)S(1)}, bf16[128,2048]{1,0:T(8,128)(2,1)}, u32[]{:S(2)}) copy-start(bf16[128,2048]{1,0:T(8,128)(2,1)} %param.8) | copy-start | bytes 1572868
  7.2 61.3 %all-gather.7.cloned.1.call-start = ((), (), s32[]{:S(2)}) async-start(), calls=%async_computation.8 | async-start | bytes 3538944 | tf_op jit(solution)/shard_map/all_gather | solution.py:38
  7.9 95.3 %all-gather.5.cloned.1.call-start = ((), (), s32[]{:S(2)}) async-start(), calls=%async_computation.7 | async-start | bytes 3538944 | tf_op jit(solution)/shard_map/all_gather | solution.py:37
  8.7 140.0 %all-gather.9.cloned.1.call-start = ((), (), s32[]{:S(2)}) async-start(), calls=%async_computation.12 | async-start | bytes 3538944 | tf_op jit(solution)/shard_map/all_gather | solution.py:36
  11.5 2.5 copy-start.4
  11.5 2.7 copy-start.5
  11.5 2.7 copy-start.6
  21.2 3.3 %copy-start.1 = (bf16[512,2048]{1,0:T(8,128)(2,1)S(1)}, bf16[512,2048]{1,0:T(8,128)(2,1)}, u32[]{:S(2)}) copy-start(bf16[512,2048]{1,0:T(8,128)(2,1)} %gather_fusion.2) | copy-start | bytes 6291460
  62.4 33.9 %all-to-all-start = ((bf16[32,16,2048]{2,1,0:T(8,128)(2,1)}), bf16[32,16,2048]{2,1,0:T(8,128)(2,1)}, u32[]{:S(2)}, u32[]{:S(2)}) async-start(bf16[32,16,2048]{2,1,0:T(8,128)(2,1)} %get-tuple-element.10), calls=%async_computation | async-start | bytes 4194304 | tf_op jit(solution)/shard_map/all_to_all | solution.py:43
  68.2 195.1 %reduce-scatter.4.cloned.1.call-start = ((), (), s32[]{:S(2)}) async-start(), calls=%async_computation.9 | async-start | bytes 3538944 | tf_op jit(solution)/shard_map/reduce_scatter | solution.py:95
  160.7 102.6 %reduce-scatter.6.cloned.1.call-start = ((), (), s32[]{:S(2)}) async-start(), calls=%async_computation.10 | async-start | bytes 3538944 | tf_op jit(solution)/shard_map/reduce_scatter | solution.py:101
  166.0 139.5 %reduce-scatter.8.cloned.1.call-start = ((), (), s32[]{:S(2)}) async-start(), calls=%async_computation.11 | async-start | bytes 3538944 | tf_op jit(solution)/shard_map/reduce_scatter | solution.py:107
  170.7 1.2 copy-start.8
  176.8 35.3 %all-to-all-start.1 = ((bf16[32,16,2048]{2,1,0:T(8,128)(2,1)}), bf16[32,16,2048]{2,1,0:T(8,128)(2,1)S(1)}, u32[]{:S(2)}, u32[]{:S(2)}) async-start(bf16[32,16,2048]{2,1,0:T(8,128)(2,1)} %bitcast.48), calls=%async_computation.1 | async-start | bytes 4194304 | tf_op jit(solution)/shard_map/all_to_all | solution.py:52
  184.3 4.1 %copy-start.7 = (bf16[8,256,768]{2,1,0:T(8,128)(2,1)S(1)}, bf16[8,256,768]{2,1,0:T(8,128)(2,1)}, u32[]{:S(2)}) copy-start(bf16[8,256,768]{2,1,0:T(8,128)(2,1)} %all-gather.9.cloned.1.call-done) | copy-start | bytes 9437188
  212.2 34.8 %all-to-all-start.3 = ((bf16[32,16,2048]{2,1,0:T(8,128)(2,1)}), bf16[32,16,2048]{2,1,0:T(8,128)(2,1)}, u32[]{:S(2)}, u32[]{:S(2)}) async-start(bf16[32,16,2048]{2,1,0:T(8,128)(2,1)} %bitcast.47), calls=%async_computation.3 | async-start | bytes 4194304 | tf_op jit(solution)/shard_map/all_to_all | solution.py:86
  251.3 1.5 copy-start.3
  252.8 3.0 copy-start.2
Sparse Core Ops, SparseCore 0:
  9.8 47.9 all-gather.6
  59.5 43.6 all-gather.4
  105.0 43.5 all-gather.8
  160.8 45.7 reduce-scatter.3
  209.5 46.3 reduce-scatter.5
  258.9 46.4 reduce-scatter.7
